TPU v7x, 128 devices: a whole 4x4x4 slice. The times are simulated.
128 devices in a mesh: tm: 64 (over z, y, x), row: 2 (over core).
Axes of the slice: x: 4, y: 4, z: 4, core: 2. Of those that a mesh axis runs over, the one named last changes fastest.
Arguments:
- transition: float32 [1024, 1024], P('row'), may hold values from -1 to 1, as said below
- gain_fwd: float32 [1024, 1024], P(None, 'row'), may hold values from -0.01171875 to 0.01171875
- gain_bwd: float32 [1024, 1024], P(None, 'row'), may hold values from -0.01171875 to 0.01171875
- blend: float32 [1024, 1024], P(None, 'row'), may hold values from -0.1875 to 0.1875
- prior_state: float32 [1024], replicated, may hold values from -6 to 6
- final_state: float32 [1024], replicated, may hold values from -6 to 6
- obs_index: int32 [2048, 128], P('tm'), may hold values from 0 to 1023
- obs_visible: int32 [2048, 128], P('tm'), may hold values 0 or 1
- obs_value: float32 [2048, 128], P('tm'), may hold values from -6 to 6
Outputs:
- smoothed: float32 [2048, 1024], P('tm', 'row')
Inputs may be any that keep to these rules, and one draw needn't show every extreme that they name: `transition`: symmetric; every eigenvalue lies strictly between 0 and 1.
All inputs are finite; a program needn't handle non-finite values. No bound on the sum of `obs_visible` on one device may be relied on, other than what follows from the above.
Results may differ from a plain program's by a relative error of at most 0.0003.
Values sent between devices are 32-bit elements; how exact they have to be, the bound alone decides.
No kernel may reach another device: no remote copies, remote signals or barrier semaphores. Data moves between devices by JAX's collectives and lax.ppermute only.
A program may use at most 128 MiB of HBM per device.

v0:
```python
import jax
import jax.numpy as jnp
from jax import lax
from jax.sharding import PartitionSpec as P


def passed_along(array, axis, by):
    length = lax.axis_size(axis)
    pairs = [(i, i + by) for i in range(length) if 0 <= i + by < length]
    return lax.ppermute(array, axis, pairs)


def square_slab(slab_rows):
    return jnp.dot(
        slab_rows,
        lax.all_gather(slab_rows, "row", axis=0, tiled=True),
        precision=lax.Precision.HIGHEST,
    )


def ladder_slabs(slab_rows, full_matrix, levels):
    slab_list = [slab_rows]
    full_list = [full_matrix]
    for level in range(1, levels + 1):
        squared = square_slab(slab_list[-1])
        slab_list.append(squared)
        if level < levels:
            full_list.append(lax.all_gather(squared, "row", axis=0, tiled=True))
    return (full_list, slab_list[levels])


def sweep(full_list, innov_fwd, innov_bwd, start_fwd, start_bwd):
    epochs = innov_fwd.shape[0]
    state_size = innov_fwd.shape[1]
    contract = (((1,), (1,)), ((), ()))
    starts = jnp.stack((start_fwd, start_bwd), axis=0)
    heads = lax.dot_general(starts, full_list[0], contract, precision=lax.Precision.HIGHEST)
    paired = jnp.stack((innov_fwd, innov_bwd[::-1]), axis=0)
    paired = paired.at[:, 0, :].add(heads)
    for level, power in enumerate(full_list):
        step_size = 1 << level
        shifted = jnp.concatenate(
            (
                jnp.zeros((2, step_size, state_size), jnp.float32),
                paired[:, : epochs - step_size, :],
            ),
            axis=1,
        )
        paired = paired + lax.dot_general(
            shifted, power, (((2,), (1,)), ((), ())), precision=lax.Precision.HIGHEST
        )
    seq_fwd = paired[0]
    seq_bwd = paired[1][::-1]
    return (seq_fwd[-1], seq_bwd[0], seq_fwd, seq_bwd)


def per_device(
    transition,
    gain_fwd,
    gain_bwd,
    blend,
    prior_state,
    final_state,
    obs_index,
    obs_visible,
    obs_value,
):
    highest = lax.Precision.HIGHEST
    slab_count = transition.shape[0]
    state_size = transition.shape[1]
    epochs = obs_index.shape[0]
    levels = (epochs - 1).bit_length()
    offset = lax.axis_index("row") * slab_count
    weights = obs_value * obs_visible.astype(jnp.float32)
    places = jnp.broadcast_to(jnp.arange(epochs, dtype=jnp.int32)[:, None], obs_index.shape)
    sparse = jnp.zeros((epochs, state_size), jnp.float32).at[places, obs_index].add(weights)
    fwd_part = jnp.dot(sparse, gain_fwd, precision=highest)
    bwd_part = jnp.dot(sparse, gain_bwd, precision=highest)
    innov_fwd, innov_bwd = (
        lax.all_gather(fwd_part, "row", axis=1, tiled=True),
        lax.all_gather(bwd_part, "row", axis=1, tiled=True),
    )
    full_matrix = lax.all_gather(transition, "row", axis=0, tiled=True)
    full_list, segment_map = ladder_slabs(transition, full_matrix, levels)
    segment_index = lax.axis_index("tm")
    segments = lax.axis_size("tm")
    nothing = jnp.zeros((state_size,), jnp.float32)
    head_fwd = jnp.where(segment_index == 0, prior_state, nothing)
    head_bwd = jnp.where(segment_index == segments - 1, final_state, nothing)
    offset_fwd, offset_bwd, _, _ = sweep(full_list, innov_fwd, innov_bwd, head_fwd, head_bwd)
    own_fwd = lax.dynamic_slice_in_dim(offset_fwd, offset, slab_count)
    own_bwd = lax.dynamic_slice_in_dim(offset_bwd, offset, slab_count)

    def chain_turn(turn_number, incoming):
        out_fwd = jnp.dot(segment_map, incoming[0], precision=highest) + own_fwd
        out_bwd = jnp.dot(segment_map, incoming[1], precision=highest) + own_bwd
        full_fwd, full_bwd = (
            lax.all_gather(out_fwd, "row", axis=0, tiled=True),
            lax.all_gather(out_bwd, "row", axis=0, tiled=True),
        )
        return (passed_along(full_fwd, "tm", 1), passed_along(full_bwd, "tm", -1))

    enter_fwd, enter_bwd = lax.fori_loop(0, segments - 1, chain_turn, (nothing, nothing))
    start_fwd = enter_fwd + head_fwd
    start_bwd = enter_bwd + head_bwd
    _, _, seq_fwd, seq_bwd = sweep(full_list, innov_fwd, innov_bwd, start_fwd, start_bwd)
    own_states = lax.dynamic_slice_in_dim(seq_fwd, offset, slab_count, 1)
    return own_states + jnp.dot(seq_bwd - seq_fwd, blend, precision=highest)


def solution(mesh):
    placed = (
        P("row", None),
        P(None, "row"),
        P(None, "row"),
        P(None, "row"),
        P(),
        P(),
        P("tm", None),
        P("tm", None),
        P("tm", None),
    )
    return jax.shard_map(
        per_device, mesh=mesh, in_specs=placed, out_specs=P("tm", "row"), check_vma=False
    )
```

profile of v0, /device:TPU:30, one launch (start us, length us, event | category | flops | bytes accessed | tf_op | source)
XLA Modules:
  0.0 1640.7 jit_solution(16681039773451250580)
XLA Ops:
  7.3 20.2 %all-gather.12.cloned.1.call-done = f32[1024,1024]{1,0:T(8,128)} async-done(((f32[512,1024]{1,0:T(8,128)}), f32[1024,1024]{1,0:T(8,128)}) %all-gather.12.cloned.1.call-update) | async-done | bytes 4194320 | tf_op jit(solution)/shard_map/all_gather | solution.py:16
  27.5 10.3 fusion.91
  37.9 17.8 %all-gather.14.cloned.1.call-done = f32[1024,1024]{1,0:T(8,128)} async-done(((f32[512,1024]{1,0:T(8,128)}), f32[1024,1024]{1,0:T(8,128)}) %all-gather.14.cloned.1.call-update) | async-done | bytes 4194320 | tf_op jit(solution)/shard_map/all_gather | solution.py:16
  55.7 10.2 fusion.92
  66.0 17.8 %all-gather.16.cloned.1.call-done = f32[1024,1024]{1,0:T(8,128)} async-done(((f32[512,1024]{1,0:T(8,128)}), f32[1024,1024]{1,0:T(8,128)}) %all-gather.16.cloned.1.call-update) | async-done | bytes 4194320 | tf_op jit(solution)/shard_map/all_gather | solution.py:16
  83.8 10.2 fusion.93
  94.4 17.5 %all-gather.18.cloned.1.call-done = f32[1024,1024]{1,0:T(8,128)} async-done(((f32[512,1024]{1,0:T(8,128)}), f32[1024,1024]{1,0:T(8,128)}) %all-gather.18.cloned.1.call-update) | async-done | bytes 4194320 | tf_op jit(solution)/shard_map/all_gather | solution.py:16
  112.0 10.2 fusion.94
  122.5 28.8 %scatter_custom_fusion = f32[32768]{0:T(1024)S(1)} fusion(s32[4096]{0:T(1024)S(1)} %select_bitcast_fusion, f32[4096]{0:T(1024)S(1)} %multiply_bitcast_fusion, f32[]{:T(128)} %constant.74.clone.1), kind=kCustom, calls=%fused_computation.47 | custom fusion | flops 4096 | bytes 131076
  165.8 6.4 fusion.20
  184.9 6.4 fusion.44
  191.4 9.8 fusion.95
  201.1 1399.5 %while.14 = (s32[]{:T(128)}, f32[1024]{0:T(1024)S(1)}, f32[1024]{0:T(1024)S(1)}, f32[512,1024]{1,0:T(8,128)}, f32[512]{0:T(512)S(1)}, /*index=5*/f32[512]{0:T(512)S(1)}, s32[]{:T(128)}) while((s32[]{:T(128)}, f32[1024]{0:T(1024)S(1)}, f32[1024]{0:T(1024)S(1)}, f32[512,1024]{1,0:T(8,128)}, f32[512]{0:T(512)S(1)}, /*index=5*/f32[512]{0:T(512)S(1)}, ...), condition=%wide.region_2.3_spmd, body=%wide.region_1.2_spmd.sunk | while | flops 12583938 | bytes 4264093 | solution.py:103
  217.5 7.2 collective-permute-done.1
  307.7 5.8 collective-permute-done.1
  329.9 5.8 collective-permute-done.1
  352.1 5.8 collective-permute-done.1
  374.3 5.8 collective-permute-done.1
  396.5 5.8 collective-permute-done.1
  418.7 5.8 collective-permute-done.1
  440.9 5.8 collective-permute-done.1
  463.1 5.8 collective-permute-done.1
  485.3 5.8 collective-permute-done.1
  1606.7 6.4 fusion.23
  (705 shorter events, 1393.3 us)
Async XLA Ops:
  6.5 21.0 %all-gather.12.cloned.1.call-start = ((), (), s32[]{:S(2)}) async-start(), calls=%async_computation | async-start | bytes 6291456 | tf_op jit(solution)/shard_map/all_gather | solution.py:16
  7.3 48.4 %all-gather.14.cloned.1.call-start = ((), (), s32[]{:S(2)}) async-start(), calls=%async_computation.1 | async-start | bytes 6291456 | tf_op jit(solution)/shard_map/all_gather | solution.py:16
  37.8 46.0 %all-gather.16.cloned.1.call-start = ((), (), s32[]{:S(2)}) async-start(), calls=%async_computation.2 | async-start | bytes 6291456 | tf_op jit(solution)/shard_map/all_gather | solution.py:16
  66.0 46.0 %all-gather.18.cloned.1.call-start = ((), (), s32[]{:S(2)}) async-start(), calls=%async_computation.3 | async-start | bytes 6291456 | tf_op jit(solution)/shard_map/all_gather | solution.py:16
  94.2 90.7 %all-gather.20.cloned.1.call-start = ((), (), s32[]{:S(2)}) async-start(), calls=%async_computation.4 | async-start | bytes 6291456 | tf_op jit(solution)/shard_map/all_gather | solution.py:16
  230.0 11.1 collective-permute-start
  252.2 11.1 collective-permute-start
  274.4 11.1 collective-permute-start
  296.6 11.1 collective-permute-start
  318.8 11.1 collective-permute-start
  341.0 11.1 collective-permute-start
  363.2 11.1 collective-permute-start
  385.4 11.1 collective-permute-start
  629.5 11.1 collective-permute-start
  651.7 11.1 collective-permute-start
  673.9 11.1 collective-permute-start
  696.1 11.1 collective-permute-start
  718.3 11.1 collective-permute-start
  740.4 11.1 collective-permute-start
  762.6 11.1 collective-permute-start
  784.8 11.1 collective-permute-start
  807.0 11.1 collective-permute-start
  1051.1 11.1 collective-permute-start
  1073.3 11.1 collective-permute-start
  (123 other events, 1527.5 us)
Sparse Core Ops, SparseCore 0:
  9.0 18.4 all-gather.11
  38.0 17.6 all-gather.13
  66.1 17.6 all-gather.15
  94.2 17.6 all-gather.17
  122.4 17.7 all-gather.19
where the time goes:
time: 1660 us; the launch traced here: 1640 us
  matrix products  551 us (33%)
  waiting for transfers between devices  440 us (27%)
  starting transfers between devices  367 us (22%)
  blocking collectives  236 us (14%)
  other arithmetic  29.8 us (2%)
    ppermute x126, starting transfers between devices, passed_along(): return lax.ppermute(array, axis, pairs)  367 us
    ppermute x126, waiting for transfers between devices, passed_along(): return lax.ppermute(array, axis, pairs)  365 us
    dot_general x63, matrix products, chain_turn(): out_bwd = jnp.dot(segment_map, incoming[1], precision=highest) + own_bwd  216 us
    dot_general x63, matrix products, chain_turn(): out_fwd = jnp.dot(segment_map, incoming[0], precision=highest) + own_fwd  216 us
    all_gather x63, blocking collectives, chain_turn(): lax.all_gather(out_fwd, 'row', axis=0, tiled=True)  116 us
    all_gather x63, blocking collectives, chain_turn(): lax.all_gather(out_bwd, 'row', axis=0, tiled=True)  116 us
    all_gather x5, waiting for transfers between devices, square_slab(): lax.all_gather(slab_rows, 'row', axis=0, tiled=True)  73.4 us
    dot_general x5, matrix products, square_slab(): jnp.dot(slab_rows, lax.all_gather(slab_rows, 'row', axis=0, tiled=True),...  50.8 us
  transfers between devices with their start and end apart: 131, of which 67 were waited for; matrix products, arithmetic and copies ran while one was open for 17% of the time, Pallas kernels for 0%

commit v1 on v0

v1 whole, which is shorter than its diff:
```python
import jax
import jax.numpy as jnp
from jax import lax
from jax.experimental import pallas as pl
from jax.experimental.pallas import tpu as pltpu
from jax.sharding import PartitionSpec as P

F = jnp.float32
B = jnp.bfloat16
S = 1024
H = 512
Q = 256
EP = 32
PAD = 16


def mm(a, b):
    return lax.dot_general(a, b, (((1,), (0,)), ((), ())), preferred_element_type=F)


def split(x):
    hi = x.astype(B)
    return hi, (x - hi.astype(F)).astype(B)


def product(x, hi, lo):
    n = x.shape[0]
    a, b = split(x)
    p = mm(jnp.concatenate((a, b), axis=0), hi)
    return p[:n] + (p[n:] + mm(a, lo))


def eye(n):
    return lax.broadcasted_iota(jnp.int32, (n, n), 0) == lax.broadcasted_iota(jnp.int32, (n, n), 1)


def low_diagonal(l, i):
    low = l[pl.ds(PAD + i * Q, Q), :].astype(F)
    return jnp.where(eye(Q), jnp.sum(low * low, axis=1, keepdims=True), 0.0)


def square(src, emit, carried, after=None):
    h, l, f = src
    for j in (3, 2, 1, 0):
        cols = pl.ds(j * Q, Q)
        hc = h[pl.ds(PAD, S), cols]
        lc = l[pl.ds(PAD, S), cols]
        for i in range(j + 1):
            rows = pl.ds(0, PAD + Q) if i == 0 and carried is not None else pl.ds(PAD + i * Q, Q)
            p = mm(h[rows, :], hc) + (mm(l[rows, :], hc) + mm(h[rows, :], lc))
            if i == 0 and carried is not None:
                carried[:, cols] = p[:PAD]
                p = p[PAD:]
            if i == j:
                p = p + low_diagonal(l, i)
            at = pl.ds(PAD + i * Q, Q)
            twice = f[pl.ds(i * Q, Q), cols] if f is not None else h[at, cols].astype(F) + l[at, cols].astype(F)
            emit(i, j, 2.0 * twice - p)
        if after is not None:
            after(j)


def put(dst):
    h, l, f = dst

    def one(i, j, d):
        if f is not None:
            f[pl.ds(i * Q, Q), pl.ds(j * Q, Q)] = d
        a, b = split(d)
        h[pl.ds(PAD + i * Q, Q), pl.ds(j * Q, Q)] = a
        l[pl.ds(PAD + i * Q, Q), pl.ds(j * Q, Q)] = b

    def both(i, j, d):
        one(i, j, d)
        if i < j:
            one(j, i, d.T)

    return both


def innovation_kernel(idx, vis, val, gf, gb, keep, send, sparse, both, gain, sem):
    r = lax.axis_index("row")
    copies = [pltpu.make_async_copy(g, gain.at[n], sem.at[n]) for n, g in enumerate((gf, gb))]
    for c in copies:
        c.start()
    low = lax.broadcasted_iota(jnp.int32, (128, 128), 0)
    high = lax.broadcasted_iota(jnp.int32, (8, 128), 0)
    for k in range(EP):
        at = idx[pl.ds(k, 1), :]
        w = val[pl.ds(k, 1), :] * vis[pl.ds(k, 1), :].astype(F)
        place = jnp.where((at & 127) == low, 1.0, 0.0).astype(B)
        part = jnp.where((at >> 7) == high, w, 0.0)
        a, b = split(part)
        rows = lax.dot_general(
            jnp.concatenate((a, b), axis=0), place, (((1,), (1,)), ((), ())), preferred_element_type=F
        )
        rows = rows[:8] + rows[8:]
        for q in range(8):
            sparse[pl.ds(k, 1), pl.ds(q * 128, 128)] = rows[q : q + 1]
    x = sparse[...]
    for n in range(2):
        copies[n].wait()
        both[n] = product(x, *split(gain[n]))

    @pl.when(r == 0)
    def _():
        keep[...] = both[0]
        for k in range(EP):
            send[pl.ds(EP - 1 - k, 1), :] = both[1, pl.ds(k, 1), :]

    @pl.when(r == 1)
    def _():
        send[...] = both[0]
        for k in range(EP):
            keep[pl.ds(EP - 1 - k, 1), :] = both[1, pl.ds(k, 1), :]


HBM = pl.BlockSpec(memory_space=pltpu.HBM)
VMEM = pl.BlockSpec(memory_space=pltpu.VMEM)


def innovation(idx, vis, val, gf, gb):
    half = jax.ShapeDtypeStruct((EP, H), F)
    return pl.pallas_call(
        innovation_kernel,
        out_shape=(half, half),
        in_specs=[VMEM, VMEM, VMEM, HBM, HBM],
        scratch_shapes=[
            pltpu.VMEM((EP, S), F),
            pltpu.VMEM((2, EP, H), F),
            pltpu.VMEM((2, S, H), F),
            pltpu.SemaphoreType.DMA((2,)),
        ],
        compiler_params=pltpu.CompilerParams(vmem_limit_bytes=62 << 20),
        name="innovation",
    )(idx, vis, val, gf, gb)


def ladder_kernel(own, recv, keep, other, ends, kh, kl, ah, al, af, ch, cl, cf, vec, vd, sem):
    r = lax.axis_index("row")
    one = jnp.where(eye(H), 1.0, 0.0)

    def fill(diag, off):
        lower = -off
        for (i, j), d in (((0, 0), one - diag), ((0, 1), lower), ((1, 0), lower.T), ((1, 1), one - recv[...])):
            a, b = split(d)
            af[pl.ds(i * H, H), pl.ds(j * H, H)] = d
            ah[pl.ds(PAD + i * H, H), pl.ds(j * H, H)] = a
            al[pl.ds(PAD + i * H, H), pl.ds(j * H, H)] = b

    @pl.when(r == 0)
    def _():
        fill(own[:, :H], own[:, H:])

    @pl.when(r == 1)
    def _():
        fill(own[:, H:], own[:, :H])

    vec[:, :H] = keep[...]
    vec[:, H:] = other[...]
    at = lax.broadcasted_iota(jnp.int32, (EP, EP), 0)
    at = 2 * (at & 15) + (at >> 4)
    parity = jnp.where(at == lax.broadcasted_iota(jnp.int32, (EP, EP), 1), 1.0, 0.0)

    def save(h, l, slot):
        copies = (
            pltpu.make_async_copy(h.at[pl.ds(PAD, S), :], kh.at[slot], sem.at[0]),
            pltpu.make_async_copy(l.at[pl.ds(PAD, S), :], kl.at[slot], sem.at[1]),
        )
        for c in copies:
            c.start()
        return copies

    def level(src, dst, slot):
        copies = save(src[0], src[1], slot)
        halves = jnp.dot(parity, vec[...], precision=lax.Precision.HIGHEST, preferred_element_type=F)
        even, odd = halves[:PAD], halves[PAD:]
        a, b = split(even)
        src[0][pl.ds(0, PAD), :] = a
        src[1][pl.ds(0, PAD), :] = b
        square(src, put(dst), vd)
        vec[pl.ds(0, PAD), :] = odd + (even - vd[...])
        for c in copies:
            c.wait()

    first, second = (ah, al, af), (ch, cl, cf)

    def two(n, _):
        level(first, second, 2 * n)
        level(second, first, 2 * n + 1)
        return 0

    lax.fori_loop(0, 2, two, 0)
    copies = save(ah, al, 4)
    tail = vec[pl.ds(0, PAD), :]
    p = product(tail, ah[pl.ds(PAD, S), :], al[pl.ds(PAD, S), :])
    end = tail[1:2] + (tail[0:1] - p[0:1])
    ends[...] = jnp.broadcast_to(end.reshape(1, 1, S), ends.shape)
    for c in copies:
        c.wait()


def ladder(own, recv, keep, other, segments):
    store = jax.ShapeDtypeStruct((5, S, S), B)
    slab = pltpu.VMEM((PAD + S, S), B)
    full = pltpu.VMEM((S, S), F)
    return pl.pallas_call(
        ladder_kernel,
        out_shape=(jax.ShapeDtypeStruct((segments, 1, S), F), store, store),
        out_specs=(VMEM, HBM, HBM),
        scratch_shapes=[slab, slab, full, slab, slab, full]
        + [pltpu.VMEM((EP, S), F), pltpu.VMEM((PAD, S), F), pltpu.SemaphoreType.DMA((2,))],
        compiler_params=pltpu.CompilerParams(vmem_limit_bytes=58 << 20),
        name="ladder",
    )(own, recv, keep, other)


def middle_kernel(kh, kl, mh, ml, ah, al, ch, cl, cf, eh, el, sem):
    loads = (
        pltpu.make_async_copy(kh.at[4], ah.at[pl.ds(PAD, S), :], sem.at[0]),
        pltpu.make_async_copy(kl.at[4], al.at[pl.ds(PAD, S), :], sem.at[1]),
    )
    for c in loads:
        c.start()
    for c in loads:
        c.wait()

    def saver(h, l, slot):
        out = []

        def save(j):
            at = pl.ds(j * Q, Q)
            for n, (a, b) in enumerate(((h, mh), (l, ml))):
                c = pltpu.make_async_copy(a.at[pl.ds(PAD + j * Q, Q), :], b.at[slot, at, :], sem.at[2 + slot * 8 + n * 4 + j])
                c.start()
                out.append(c)

        return save, out

    save, first = saver(ch, cl, 0)
    square((ah, al, None), put((ch, cl, cf)), None, save)
    save, second = saver(eh, el, 1)
    square((ch, cl, cf), put((eh, el, None)), None, save)
    for c in first + second:
        c.wait()


def middle(kh, kl):
    store = jax.ShapeDtypeStruct((2, S, S), B)
    slab = pltpu.VMEM((PAD + S, S), B)
    return pl.pallas_call(
        middle_kernel,
        out_shape=(store, store),
        in_specs=[HBM, HBM],
        out_specs=(HBM, HBM),
        scratch_shapes=[slab, slab, slab, slab, pltpu.VMEM((S, S), F), slab, slab, pltpu.SemaphoreType.DMA((18,))],
        compiler_params=pltpu.CompilerParams(vmem_limit_bytes=61 << 20),
        name="middle",
    )(kh, kl)


def sweep_kernel(
    got, prior, final, keep, other, kh, kl, mh, ml,
    out, sh, sl, ch, cl, eh, el, mat, rows, vd, state, sem,
):
    r = lax.axis_index("row")
    seg = lax.axis_index("tm")
    segments = got.shape[0]

    def load(n, hs, ls, hd, ld):
        copies = (pltpu.make_async_copy(hs, hd, sem.at[0, n]), pltpu.make_async_copy(ls, ld, sem.at[1, n]))
        for c in copies:
            c.start()
        return copies

    body = pl.ds(PAD, S)
    last = load(6, mh.at[1], ml.at[1], eh.at[body, :], el.at[body, :])
    pair = load(5, mh.at[0], ml.at[0], ch, cl)
    small = [load(n, kh.at[n], kl.at[n], sh.at[n], sl.at[n]) for n in range(5)]
    sign = 2 * r - 1
    before = jnp.where(r == 0, seg, segments - 1 - seg)
    start = jnp.where(r == 0, prior[...], jnp.concatenate((final[:, H:], final[:, :H]), axis=1))

    def order(shape):
        a = lax.broadcasted_iota(jnp.int32, shape, 0)
        t = jnp.where((a & 31) < 16, 2 * (a & 15), 2 * (a & 15) + 1)
        return 2 * t + (a >> 5)

    for n in range(segments):
        rows[pl.ds(n, 1), :] = got[n]
    q = order((64, segments))
    pick = jnp.where(lax.broadcasted_iota(jnp.int32, (64, segments), 1) == seg + sign * (q + 1), 1.0, 0.0)
    terms = jnp.dot(pick, rows[...], precision=lax.Precision.HIGHEST, preferred_element_type=F)
    terms = terms + jnp.where(order((64, 1)) == before, 1.0, 0.0) * start
    near, far = terms[:32], terms[32:]
    for c in last + pair:
        c.wait()
    pairs = near + (far - product(far, ch[...], cl[...]))
    near, far = pairs[:16], pairs[16:]
    a, b = split(far)
    eh[pl.ds(0, PAD), :] = a
    el[pl.ds(0, PAD), :] = b

    def emit(i, j, d):
        m = jnp.where(eye(Q), 1.0, 0.0) - d if i == j else -d
        mat[pl.ds(i * Q, Q), pl.ds(j * Q, Q)] = m
        if i < j:
            mat[pl.ds(j * Q, Q), pl.ds(i * Q, Q)] = m.T

    square((eh, el, None), emit, vd)
    quads = near + (far - vd[...])
    vd[...] = quads
    lane = lax.broadcasted_iota(jnp.int32, (1, 128), 1)
    mat[:, pl.ds(S, 128)] = jnp.concatenate((quads, jnp.zeros((128 - PAD, S), F)), axis=0).T

    def two(u, z):
        s = PAD - 1 - 2 * u
        wide = jnp.concatenate((z, jnp.where(lane == s, 1.0, 0.0)), axis=1)
        col = jnp.sum(mat[...] * wide, axis=1, keepdims=True)
        return vd[pl.ds(s - 1, 1), :] + jnp.sum(mat[:, pl.ds(0, S)] * col, axis=0, keepdims=True)

    z = lax.fori_loop(0, PAD // 2, two, jnp.zeros((1, S), F))
    state[:, :H] = keep[...]
    state[:, H:] = other[...]
    z8 = jnp.broadcast_to(z, (8, S))
    for c in small[0]:
        c.wait()
    head = z8 - product(z8, sh[0], sl[0])
    state[pl.ds(0, 1), :] = state[pl.ds(0, 1), :] + head[0:1]
    for n in range(5):
        step = 1 << n
        if n:
            for c in small[n]:
                c.wait()
        x = state[...]
        moved = x - product(x, sh[n], sl[n])
        state[pl.ds(step, EP - step), :] = x[step:] + moved[: EP - step]

    @pl.when(r == 0)
    def _():
        out[...] = state[...]

    @pl.when(r == 1)
    def _():
        for k in range(EP):
            out[pl.ds(EP - 1 - k, 1), :] = state[pl.ds(k, 1), :]


def sweep(got, prior, final, keep, other, kh, kl, mh, ml):
    slab = pltpu.VMEM((PAD + S, S), B)
    mats = pltpu.VMEM((S, S), B)
    return pl.pallas_call(
        sweep_kernel,
        out_shape=jax.ShapeDtypeStruct((EP, S), F),
        in_specs=[VMEM] * 5 + [HBM] * 4,
        out_specs=VMEM,
        scratch_shapes=[
            pltpu.VMEM((5, S, S), B),
            pltpu.VMEM((5, S, S), B),
            mats,
            mats,
            slab,
            slab,
            pltpu.VMEM((S, S + 128), F),
            pltpu.VMEM((got.shape[0], S), F),
            pltpu.VMEM((PAD, S), F),
            pltpu.VMEM((EP, S), F),
            pltpu.SemaphoreType.DMA((2, 7)),
        ],
        compiler_params=pltpu.CompilerParams(vmem_limit_bytes=60 << 20),
        name="sweep",
    )(got, prior, final, keep, other, kh, kl, mh, ml)


def blend_kernel(mine, theirs, blend, out):
    r = lax.axis_index("row")
    swapped = jnp.concatenate((theirs[:, H:], theirs[:, :H]), axis=1)
    own = mine[...]
    fwd = jnp.where(r == 0, own, swapped)
    bwd = jnp.where(r == 0, swapped, own)
    gap = bwd - fwd
    total = fwd[:, :H]
    for n, place in enumerate((r, 1 - r)):
        hi, lo = split(blend[pl.ds(pl.multiple_of(place * H, H), H), :])
        total = total + product(gap[:, n * H : (n + 1) * H], hi, lo)
    out[...] = total


def blended(mine, theirs, blend):
    return pl.pallas_call(
        blend_kernel,
        out_shape=jax.ShapeDtypeStruct((EP, H), F),
        compiler_params=pltpu.CompilerParams(vmem_limit_bytes=4 << 20),
        name="blended",
    )(mine, theirs, blend)


def per_device(
    transition, gain_fwd, gain_bwd, blend, prior_state, final_state, obs_index, obs_visible, obs_value
):
    r = lax.axis_index("row")
    segments = lax.axis_size("tm")
    swap = [(0, 1), (1, 0)]
    diag = lax.dynamic_slice_in_dim(transition, r * H, H, 1)
    recv = lax.ppermute(diag, "row", swap)
    keep, send = innovation(obs_index, obs_visible, obs_value, gain_fwd, gain_bwd)
    other = lax.ppermute(send, "row", swap)
    ends, kh, kl = ladder(transition, recv, keep, other, segments)
    got = lax.all_to_all(ends, "tm", 0, 0)
    mh, ml = middle(kh, kl)
    states = sweep(got, prior_state.reshape(1, S), final_state.reshape(1, S), keep, other, kh, kl, mh, ml)
    theirs = lax.ppermute(states, "row", swap)
    return blended(states, theirs, blend)


def solution(mesh):
    placed = (
        P("row", None),
        P(None, "row"),
        P(None, "row"),
        P(None, "row"),
        P(),
        P(),
        P("tm", None),
        P("tm", None),
        P("tm", None),
    )
    return jax.shard_map(
        per_device, mesh=mesh, in_specs=placed, out_specs=P("tm", "row"), check_vma=False
    )
```

time: 1660 us -> 85.9 us (0.05)
  the two profiles are of different devices: /device:TPU:30 before, /device:TPU:1 now
where the time goes in v1:
time: 85.9 us; the launch traced here: 85.6 us
  Pallas kernels  64.6 us (75%)
  starting transfers between devices  13.4 us (16%)
  local copies, waits for them, and re-layouts  4.85 us (6%)
  waiting for transfers between devices  2.65 us (3%)
    pallas_call x1, Pallas kernels, ladder(): pl.pallas_call(ladder_kernel, out_shape=(jax.ShapeDtypeStruct((segments,...  25.4 us
    pallas_call x1, Pallas kernels, sweep(): pl.pallas_call(sweep_kernel, out_shape=jax.ShapeDtypeStruct((EP, S), F),...  20.6 us
    pallas_call x1, Pallas kernels, middle(): pl.pallas_call(middle_kernel, out_shape=(store, store), in_specs=[HBM, HB...  13.3 us
    all_to_all x1, starting transfers between devices, per_device(): got = lax.all_to_all(ends, 'tm', 0, 0)  11.5 us
    pallas_call x1, Pallas kernels, innovation(): pl.pallas_call(innovation_kernel, out_shape=(half, half), in_specs=[VMEM,...  4.17 us
    unnamed x10, local copies, waits for them, and re-layouts  2.59 us
    dynamic_slice x1, local copies, waits for them, and re-layouts, per_device(): diag = lax.dynamic_slice_in_dim(transition, r * H, H, 1)  2.27 us
  transfers between devices with their start and end apart: 4, of which 2 were waited for; matrix products, arithmetic and copies ran while one was open for 0% of the time, Pallas kernels for 20%

profile of v1, /device:TPU:1, one launch (start us, length us, event | category | flops | bytes accessed | tf_op | source)
XLA Modules:
  0.0 85.6 jit_solution(16212889424191936543)
XLA Ops:
  0.0 2.3 %constant_dynamic-slice_fusion = f32[512,512]{1,0:T(8,128)} fusion(f32[512,1024]{1,0:T(8,128)} %own.1, s32[]{:T(128)S(6)} %select_n.3), kind=kLoop, calls=%fused_computation | loop fusion | bytes 2097156 | tf_op jit(solution)/shard_map/dynamic_slice | solution.py:404
  2.3 1.4 %collective-permute-start = (f32[512,512]{1,0:T(8,128)}, f32[512,512]{1,0:T(8,128)S(1)}, u32[]{:S(2)}, u32[]{:S(2)}) collective-permute-start(f32[512,512]{1,0:T(8,128)} %constant_dynamic-slice_fusion), channel_id=1, source_target_pairs={{0,1},{1,0},{2,3},{3,2},{4,5},{5,4},{6,7},{7,6},{8,9},{9,8},{10,11... | collective-permute-start | bytes 3145736 | tf_op jit(solution)/shard_map/ppermute | solution.py:405
  3.6 4.2 %innovation.1 = (f32[32,512]{1,0:T(8,128)}, f32[32,512]{1,0:T(8,128)}) custom-call(s32[32,128]{1,0:T(8,128)} %idx.1, s32[32,128]{1,0:T(8,128)} %vis.1, f32[32,128]{1,0:T(8,128)} %val.1, f32[1024,512]{1,0:T(8,128)} %gf.1, f32[1024,512]{1,0:T(8,128)} %gb.1), custom_call_target="tpu_custom_call" | custom-call | tf_op jit(solution)/shard_map/innovation/pallas_call | solution.py:124
  7.8 0.1 collective-permute-start.1
  7.9 1.5 %collective-permute-done.1.other = f32[32,512]{1,0:T(8,128)S(1)} collective-permute-done((f32[32,512]{1,0:T(8,128)}, f32[32,512]{1,0:T(8,128)S(1)}, u32[]{:S(2)}, u32[]{:S(2)}) %collective-permute-start.1) | collective-permute-done | bytes 65568 | tf_op jit(solution)/shard_map/ppermute | solution.py:407
  9.4 0.0 copy-start.4
  9.4 0.0 collective-permute-done.recv
  9.4 0.0 copy-start.3
  9.4 0.6 copy-done.4
  10.0 0.4 copy-done.3
  10.4 25.4 %ladder.1 = (f32[64,1,1024]{2,1,0:T(1,128)}, bf16[5,1024,1024]{2,1,0:T(8,128)(2,1)}, bf16[5,1024,1024]{2,1,0:T(8,128)(2,1)}) custom-call(f32[512,1024]{1,0:T(8,128)} %own.1, f32[512,512]{1,0:T(8,128)} %copy-done.3, f32[32,512]{1,0:T(8,128)} %get-tuple-element.12.keep, f32[32,512]{1,0:T(8,128)} %copy-done.4), custom_call_target="tpu_custom_call" | custom-call | tf_op jit(solution)/shard_map/ladder/pallas_call | solution.py:207
  35.8 11.5 %all-to-all-start = ((f32[64,1,1024]{2,1,0:T(1,128)}), f32[64,1,1024]{2,1,0:T(1,128)S(1)}, u32[]{:S(2)}, u32[]{:S(2)}) async-start(f32[64,1,1024]{2,1,0:T(1,128)} %get-tuple-element.14), calls=%async_computation | async-start | bytes 524288 | tf_op jit(solution)/shard_map/all_to_all | solution.py:409
  47.3 13.3 %middle.1 = (bf16[2,1024,1024]{2,1,0:T(8,128)(2,1)}, bf16[2,1024,1024]{2,1,0:T(8,128)(2,1)}) custom-call(bf16[5,1024,1024]{2,1,0:T(8,128)(2,1)} %get-tuple-element.15.kh, bf16[5,1024,1024]{2,1,0:T(8,128)(2,1)} %get-tuple-element.16.kl), custom_call_target="tpu_custom_call" | custom-call | tf_op jit(solution)/shard_map/middle/pallas_call | solution.py:251
  60.6 0.0 all-to-all-done.got
  60.6 0.0 copy-start.2
  60.6 0.7 copy-done.2
  61.3 0.0 copy-start
  61.3 20.6 %sweep.1.mine = f32[32,1024]{1,0:T(8,128)} custom-call(f32[64,1,1024]{2,1,0:T(1,128)} %copy-done.2, f32[1,1024]{1,0:T(1,128)} %bitcast.2, f32[1,1024]{1,0:T(1,128)} %bitcast.3, f32[32,512]{1,0:T(8,128)} %get-tuple-element.12.keep, f32[32,512]{1,0:T(8,128)} %copy-done.4, bf16[5,1024,1024]{2,1,0:T(8,128)(2,1)} %get-tuple-element.15.kh, ...), custom_call_target="tpu_custom_call" | custom-call | tf_op jit(solution)/shard_map/sweep/pallas_call | solution.py:352
  81.9 0.5 collective-permute-start.2
  82.4 1.2 %collective-permute-done.2.theirs = f32[32,1024]{1,0:T(8,128)S(1)} collective-permute-done((f32[32,1024]{1,0:T(8,128)}, f32[32,1024]{1,0:T(8,128)S(1)}, u32[]{:S(2)}, u32[]{:S(2)}) %collective-permute-start.2) | collective-permute-done | bytes 131104 | tf_op jit(solution)/shard_map/ppermute | solution.py:412
  83.6 0.0 copy-done
  83.6 0.0 copy-start.1
  83.6 0.9 %copy-done.1 = f32[32,1024]{1,0:T(8,128)S(1)} copy-done((f32[32,1024]{1,0:T(8,128)S(1)}, f32[32,1024]{1,0:T(8,128)}, u32[]{:S(2)}) %copy-start.1) | copy-done | bytes 131096
  84.5 1.1 %blended.1 = f32[32,512]{1,0:T(8,128)} custom-call(f32[32,1024]{1,0:T(8,128)S(1)} %copy-done.1, f32[32,1024]{1,0:T(8,128)S(1)} %collective-permute-done.2.theirs, f32[1024,512]{1,0:T(8,128)S(1)} %copy-done), custom_call_target="tpu_custom_call" | custom-call | tf_op jit(solution)/shard_map/blended/pallas_call | solution.py:390
Async XLA Ops:
  2.3 7.1 %collective-permute-start = (f32[512,512]{1,0:T(8,128)}, f32[512,512]{1,0:T(8,128)S(1)}, u32[]{:S(2)}, u32[]{:S(2)}) collective-permute-start(f32[512,512]{1,0:T(8,128)} %constant_dynamic-slice_fusion), channel_id=1, source_target_pairs={{0,1},{1,0},{2,3},{3,2},{4,5},{5,4},{6,7},{7,6},{8,9},{9,8},{10,11... | collective-permute-start | bytes 3145736 | tf_op jit(solution)/shard_map/ppermute | solution.py:405
  7.8 1.5 %collective-permute-start.1 = (f32[32,512]{1,0:T(8,128)}, f32[32,512]{1,0:T(8,128)S(1)}, u32[]{:S(2)}, u32[]{:S(2)}) collective-permute-start(f32[32,512]{1,0:T(8,128)} %get-tuple-element.13), channel_id=1, source_target_pairs={{0,1},{1,0},{2,3},{3,2},{4,5},{5,4},{6,7},{7,6},{8,9},{9,8},{10,11... | collective-permute-start | bytes 196616 | tf_op jit(solution)/shard_map/ppermute | solution.py:407
  9.4 0.6 copy-start.4
  9.4 1.0 %copy-start.3 = (f32[512,512]{1,0:T(8,128)}, f32[512,512]{1,0:T(8,128)S(1)}, u32[]{:S(2)}) copy-start(f32[512,512]{1,0:T(8,128)S(1)} %collective-permute-done.recv) | copy-start | bytes 3145732
  35.8 24.8 %all-to-all-start = ((f32[64,1,1024]{2,1,0:T(1,128)}), f32[64,1,1024]{2,1,0:T(1,128)S(1)}, u32[]{:S(2)}, u32[]{:S(2)}) async-start(f32[64,1,1024]{2,1,0:T(1,128)} %get-tuple-element.14), calls=%async_computation | async-start | bytes 524288 | tf_op jit(solution)/shard_map/all_to_all | solution.py:409
  60.6 0.7 copy-start.2
  61.3 22.3 %copy-start = (f32[1024,512]{1,0:T(8,128)S(1)}, f32[1024,512]{1,0:T(8,128)}, u32[]{:S(2)}) copy-start(f32[1024,512]{1,0:T(8,128)} %blend.1) | copy-start | bytes 6291460
  81.9 1.7 %collective-permute-start.2 = (f32[32,1024]{1,0:T(8,128)}, f32[32,1024]{1,0:T(8,128)S(1)}, u32[]{:S(2)}, u32[]{:S(2)}) collective-permute-start(f32[32,1024]{1,0:T(8,128)} %sweep.1.mine), channel_id=1, source_target_pairs={{0,1},{1,0},{2,3},{3,2},{4,5},{5,4},{6,7},{7,6},{8,9},{9,8},{10,11... | collective-permute-start | bytes 393224 | tf_op jit(solution)/shard_map/ppermute | solution.py:412
  83.6 0.9 %copy-start.1 = (f32[32,1024]{1,0:T(8,128)S(1)}, f32[32,1024]{1,0:T(8,128)}, u32[]{:S(2)}) copy-start(f32[32,1024]{1,0:T(8,128)} %sweep.1.mine) | copy-start | bytes 393220

commit v2 on v1

--- a/solution.py
+++ b/solution.py
@@ -18,6 +18,10 @@
     return lax.dot_general(a, b, (((1,), (0,)), ((), ())), preferred_element_type=F)
 
 
+def nt(a, b):
+    return lax.dot_general(a, b, (((1,), (1,)), ((), ())), preferred_element_type=F)
+
+
 def split(x):
     hi = x.astype(B)
     return hi, (x - hi.astype(F)).astype(B)
@@ -35,29 +39,37 @@
 
 
 def low_diagonal(l, i):
-    low = l[pl.ds(PAD + i * Q, Q), :].astype(F)
-    return jnp.where(eye(Q), jnp.sum(low * low, axis=1, keepdims=True), 0.0)
-
-
-def square(src, emit, carried, after=None):
+    low = l[pl.ds(PAD, S), pl.ds(i * Q, Q)].astype(F)
+    return jnp.where(eye(Q), jnp.sum(low * low, axis=0, keepdims=True), 0.0)
+
+
+def square(src, emit, carried, order=(3, 2, 1, 0), before=None, after=None):
     h, l, f = src
-    for j in (3, 2, 1, 0):
+    for j in order:
+        if before is not None:
+            before(j)
+        right = pl.ds(PAD + j * Q, Q)
+        hc = h[right, :]
+        lc = l[right, :]
         cols = pl.ds(j * Q, Q)
-        hc = h[pl.ds(PAD, S), cols]
-        lc = l[pl.ds(PAD, S), cols]
         for i in range(j + 1):
             rows = pl.ds(0, PAD + Q) if i == 0 and carried is not None else pl.ds(PAD + i * Q, Q)
-            p = mm(h[rows, :], hc) + (mm(l[rows, :], hc) + mm(h[rows, :], lc))
+            p = nt(h[rows, :], hc) + (nt(l[rows, :], hc) + nt(h[rows, :], lc))
             if i == 0 and carried is not None:
                 carried[:, cols] = p[:PAD]
                 p = p[PAD:]
+            at = pl.ds(PAD + i * Q, Q)
             if i == j:
-                p = p + low_diagonal(l, i)
-            at = pl.ds(PAD + i * Q, Q)
+                low = l[right, :].astype(F) if before is not None else None
+                p = p + (low_diagonal(l, i) if low is None else row_diagonal(low))
             twice = f[pl.ds(i * Q, Q), cols] if f is not None else h[at, cols].astype(F) + l[at, cols].astype(F)
             emit(i, j, 2.0 * twice - p)
         if after is not None:
             after(j)
+
+
+def row_diagonal(low):
+    return jnp.where(eye(Q), jnp.sum(low * low, axis=1, keepdims=True), 0.0)
 
 
 def put(dst):
@@ -78,7 +90,7 @@
     return both
 
 
-def innovation_kernel(idx, vis, val, gf, gb, keep, send, sparse, both, gain, sem):
+def innovation_kernel(slots, gf, gb, keep, send, sparse, both, gain, sem):
     r = lax.axis_index("row")
     copies = [pltpu.make_async_copy(g, gain.at[n], sem.at[n]) for n, g in enumerate((gf, gb))]
     for c in copies:
@@ -86,8 +98,8 @@
     low = lax.broadcasted_iota(jnp.int32, (128, 128), 0)
     high = lax.broadcasted_iota(jnp.int32, (8, 128), 0)
     for k in range(EP):
-        at = idx[pl.ds(k, 1), :]
-        w = val[pl.ds(k, 1), :] * vis[pl.ds(k, 1), :].astype(F)
+        w = slots[0, pl.ds(k, 1), :]
+        at = slots[1, pl.ds(k, 1), :].astype(jnp.int32)
         place = jnp.where((at & 127) == low, 1.0, 0.0).astype(B)
         part = jnp.where((at >> 7) == high, w, 0.0)
         a, b = split(part)
@@ -119,24 +131,24 @@
 VMEM = pl.BlockSpec(memory_space=pltpu.VMEM)
 
 
-def innovation(idx, vis, val, gf, gb):
+def innovation(slots, gf, gb):
     half = jax.ShapeDtypeStruct((EP, H), F)
     return pl.pallas_call(
         innovation_kernel,
         out_shape=(half, half),
-        in_specs=[VMEM, VMEM, VMEM, HBM, HBM],
+        in_specs=[VMEM, HBM, HBM],
         scratch_shapes=[
             pltpu.VMEM((EP, S), F),
             pltpu.VMEM((2, EP, H), F),
             pltpu.VMEM((2, S, H), F),
             pltpu.SemaphoreType.DMA((2,)),
         ],
-        compiler_params=pltpu.CompilerParams(vmem_limit_bytes=62 << 20),
+        compiler_params=pltpu.CompilerParams(vmem_limit_bytes=50 << 20),
         name="innovation",
-    )(idx, vis, val, gf, gb)
-
-
-def ladder_kernel(own, recv, keep, other, ends, kh, kl, ah, al, af, ch, cl, cf, vec, vd, sem):
+    )(slots, gf, gb)
+
+
+def ladder_kernel(own, recv, keep, other, ends, store, ah, al, af, ch, cl, cf, vec, vd, sem):
     r = lax.axis_index("row")
     one = jnp.where(eye(H), 1.0, 0.0)
 
@@ -162,106 +174,129 @@
     at = 2 * (at & 15) + (at >> 4)
     parity = jnp.where(at == lax.broadcasted_iota(jnp.int32, (EP, EP), 1), 1.0, 0.0)
 
-    def save(h, l, slot):
-        copies = (
-            pltpu.make_async_copy(h.at[pl.ds(PAD, S), :], kh.at[slot], sem.at[0]),
-            pltpu.make_async_copy(l.at[pl.ds(PAD, S), :], kl.at[slot], sem.at[1]),
-        )
-        for c in copies:
+    first, second = (ah, al, af), (ch, cl, cf)
+
+    def saves(src, slot, j):
+        n = 0 if src is first else 8
+        at = pl.ds(j * Q, Q)
+        return [
+            pltpu.make_async_copy(src[m].at[pl.ds(PAD + j * Q, Q), :], store.at[5 * m + slot, at, :], sem.at[n + m * 4 + j])
+            for m in range(2)
+        ]
+
+    def start(src, slot, j):
+        for c in saves(src, slot, j):
             c.start()
-        return copies
+
+    def finish(src, slot):
+        for j in range(4):
+            for c in saves(src, slot, j):
+                c.wait()
 
     def level(src, dst, slot):
-        copies = save(src[0], src[1], slot)
         halves = jnp.dot(parity, vec[...], precision=lax.Precision.HIGHEST, preferred_element_type=F)
         even, odd = halves[:PAD], halves[PAD:]
         a, b = split(even)
         src[0][pl.ds(0, PAD), :] = a
         src[1][pl.ds(0, PAD), :] = b
-        square(src, put(dst), vd)
+        square(src, put(dst), vd, after=lambda j: start(dst, slot, j))
         vec[pl.ds(0, PAD), :] = odd + (even - vd[...])
-        for c in copies:
-            c.wait()
-
-    first, second = (ah, al, af), (ch, cl, cf)
+
+    for j in range(4):
+        start(first, 0, j)
 
     def two(n, _):
-        level(first, second, 2 * n)
-        level(second, first, 2 * n + 1)
+        level(first, second, 2 * n + 1)
+        finish(first, 2 * n)
+        level(second, first, 2 * n + 2)
+        finish(second, 2 * n + 1)
         return 0
 
     lax.fori_loop(0, 2, two, 0)
-    copies = save(ah, al, 4)
     tail = vec[pl.ds(0, PAD), :]
     p = product(tail, ah[pl.ds(PAD, S), :], al[pl.ds(PAD, S), :])
     end = tail[1:2] + (tail[0:1] - p[0:1])
     ends[...] = jnp.broadcast_to(end.reshape(1, 1, S), ends.shape)
-    for c in copies:
-        c.wait()
+    finish(first, 4)
 
 
 def ladder(own, recv, keep, other, segments):
-    store = jax.ShapeDtypeStruct((5, S, S), B)
+    store = jax.ShapeDtypeStruct((10, S, S), B)
     slab = pltpu.VMEM((PAD + S, S), B)
     full = pltpu.VMEM((S, S), F)
     return pl.pallas_call(
         ladder_kernel,
-        out_shape=(jax.ShapeDtypeStruct((segments, 1, S), F), store, store),
-        out_specs=(VMEM, HBM, HBM),
+        out_shape=(jax.ShapeDtypeStruct((segments, 1, S), F), store),
+        out_specs=(VMEM, HBM),
         scratch_shapes=[slab, slab, full, slab, slab, full]
-        + [pltpu.VMEM((EP, S), F), pltpu.VMEM((PAD, S), F), pltpu.SemaphoreType.DMA((2,))],
-        compiler_params=pltpu.CompilerParams(vmem_limit_bytes=58 << 20),
+        + [pltpu.VMEM((EP, S), F), pltpu.VMEM((PAD, S), F), pltpu.SemaphoreType.DMA((16,))],
+        compiler_params=pltpu.CompilerParams(vmem_limit_bytes=52 << 20),
         name="ladder",
     )(own, recv, keep, other)
 
 
-def middle_kernel(kh, kl, mh, ml, ah, al, ch, cl, cf, eh, el, sem):
-    loads = (
-        pltpu.make_async_copy(kh.at[4], ah.at[pl.ds(PAD, S), :], sem.at[0]),
-        pltpu.make_async_copy(kl.at[4], al.at[pl.ds(PAD, S), :], sem.at[1]),
-    )
-    for c in loads:
-        c.start()
-    for c in loads:
-        c.wait()
+def arriving(hs, ls, hd, ld, sem):
+    copies = []
+    for j in range(4):
+        at, to = pl.ds(j * Q, Q), pl.ds(PAD + j * Q, Q)
+        copies.append(
+            (
+                pltpu.make_async_copy(hs.at[at, :], hd.at[to, :], sem.at[0, j]),
+                pltpu.make_async_copy(ls.at[at, :], ld.at[to, :], sem.at[1, j]),
+            )
+        )
+        for c in copies[j]:
+            c.start()
+
+    def ready(j):
+        for c in copies[j]:
+            c.wait()
+
+    return ready
+
+
+def middle_kernel(powers, more, ah, al, ch, cl, cf, eh, el, sem, come):
+    ready = arriving(powers.at[4], powers.at[9], ah, al, come)
 
     def saver(h, l, slot):
         out = []
 
         def save(j):
             at = pl.ds(j * Q, Q)
-            for n, (a, b) in enumerate(((h, mh), (l, ml))):
-                c = pltpu.make_async_copy(a.at[pl.ds(PAD + j * Q, Q), :], b.at[slot, at, :], sem.at[2 + slot * 8 + n * 4 + j])
+            for n, a in enumerate((h, l)):
+                c = pltpu.make_async_copy(a.at[pl.ds(PAD + j * Q, Q), :], more.at[2 * n + slot, at, :], sem.at[slot * 8 + n * 4 + j])
                 c.start()
                 out.append(c)
 
         return save, out
 
+    square((ah, al, None), put((ch, cl, cf)), None, (0, 1, 2, 3), ready)
     save, first = saver(ch, cl, 0)
-    square((ah, al, None), put((ch, cl, cf)), None, save)
+    for j in range(4):
+        save(j)
     save, second = saver(eh, el, 1)
-    square((ch, cl, cf), put((eh, el, None)), None, save)
+    square((ch, cl, cf), put((eh, el, None)), None, after=save)
     for c in first + second:
         c.wait()
 
 
-def middle(kh, kl):
-    store = jax.ShapeDtypeStruct((2, S, S), B)
+def middle(powers):
     slab = pltpu.VMEM((PAD + S, S), B)
     return pl.pallas_call(
         middle_kernel,
-        out_shape=(store, store),
-        in_specs=[HBM, HBM],
-        out_specs=(HBM, HBM),
-        scratch_shapes=[slab, slab, slab, slab, pltpu.VMEM((S, S), F), slab, slab, pltpu.SemaphoreType.DMA((18,))],
-        compiler_params=pltpu.CompilerParams(vmem_limit_bytes=61 << 20),
+        out_shape=jax.ShapeDtypeStruct((6, S, S), B),
+        in_specs=[HBM],
+        out_specs=HBM,
+        scratch_shapes=[slab, slab, slab, slab, pltpu.VMEM((S, S), F), slab, slab]
+        + [pltpu.SemaphoreType.DMA((16,)), pltpu.SemaphoreType.DMA((2, 4))],
+        compiler_params=pltpu.CompilerParams(vmem_limit_bytes=52 << 20),
         name="middle",
-    )(kh, kl)
+    )(powers)
 
 
 def sweep_kernel(
-    got, prior, final, keep, other, kh, kl, mh, ml,
-    out, sh, sl, ch, cl, eh, el, mat, rows, vd, state, sem,
+    got, prior, final, keep, other, powers, more,
+    out, sh, sl, ch, cl, eh, el, mat, rows, vd, state, sem, come,
 ):
     r = lax.axis_index("row")
     seg = lax.axis_index("tm")
@@ -273,10 +308,8 @@
             c.start()
         return copies
 
-    body = pl.ds(PAD, S)
-    last = load(6, mh.at[1], ml.at[1], eh.at[body, :], el.at[body, :])
-    pair = load(5, mh.at[0], ml.at[0], ch, cl)
-    small = [load(n, kh.at[n], kl.at[n], sh.at[n], sl.at[n]) for n in range(5)]
+    ready = arriving(more.at[1], more.at[3], eh, el, come)
+    loads = {}
     sign = 2 * r - 1
     before = jnp.where(r == 0, seg, segments - 1 - seg)
     start = jnp.where(r == 0, prior[...], jnp.concatenate((final[:, H:], final[:, :H]), axis=1))
@@ -293,13 +326,6 @@
     terms = jnp.dot(pick, rows[...], precision=lax.Precision.HIGHEST, preferred_element_type=F)
     terms = terms + jnp.where(order((64, 1)) == before, 1.0, 0.0) * start
     near, far = terms[:32], terms[32:]
-    for c in last + pair:
-        c.wait()
-    pairs = near + (far - product(far, ch[...], cl[...]))
-    near, far = pairs[:16], pairs[16:]
-    a, b = split(far)
-    eh[pl.ds(0, PAD), :] = a
-    el[pl.ds(0, PAD), :] = b
 
     def emit(i, j, d):
         m = jnp.where(eye(Q), 1.0, 0.0) - d if i == j else -d
@@ -307,8 +333,26 @@
         if i < j:
             mat[pl.ds(j * Q, Q), pl.ds(i * Q, Q)] = m.T
 
-    square((eh, el, None), emit, vd)
-    quads = near + (far - vd[...])
+    def fetch(n):
+        loads[n] = load(n, powers.at[n], powers.at[5 + n], sh.at[n], sl.at[n])
+
+    def before_block(j):
+        ready(j)
+        if j == 1:
+            loads[5] = load(5, more.at[0], more.at[2], ch, cl)
+        if j == 3:
+            fetch(0)
+            fetch(1)
+
+    square((eh, el, None), emit, None, (0, 1, 2, 3), before_block)
+    for c in loads[5]:
+        c.wait()
+    fetch(2)
+    fetch(3)
+    fetch(4)
+    pairs = near + (far - product(far, ch[...], cl[...]))
+    near, far = pairs[:16], pairs[16:]
+    quads = near + (far - product(far, eh[pl.ds(PAD, S), :], el[pl.ds(PAD, S), :]))
     vd[...] = quads
     lane = lax.broadcasted_iota(jnp.int32, (1, 128), 1)
     mat[:, pl.ds(S, 128)] = jnp.concatenate((quads, jnp.zeros((128 - PAD, S), F)), axis=0).T
@@ -323,14 +367,14 @@
     state[:, :H] = keep[...]
     state[:, H:] = other[...]
     z8 = jnp.broadcast_to(z, (8, S))
-    for c in small[0]:
+    for c in loads[0]:
         c.wait()
     head = z8 - product(z8, sh[0], sl[0])
     state[pl.ds(0, 1), :] = state[pl.ds(0, 1), :] + head[0:1]
     for n in range(5):
         step = 1 << n
         if n:
-            for c in small[n]:
+            for c in loads[n]:
                 c.wait()
         x = state[...]
         moved = x - product(x, sh[n], sl[n])
@@ -346,13 +390,13 @@
             out[pl.ds(EP - 1 - k, 1), :] = state[pl.ds(k, 1), :]
 
 
-def sweep(got, prior, final, keep, other, kh, kl, mh, ml):
+def sweep(got, prior, final, keep, other, powers, more):
     slab = pltpu.VMEM((PAD + S, S), B)
     mats = pltpu.VMEM((S, S), B)
     return pl.pallas_call(
         sweep_kernel,
         out_shape=jax.ShapeDtypeStruct((EP, S), F),
-        in_specs=[VMEM] * 5 + [HBM] * 4,
+        in_specs=[VMEM] * 5 + [HBM] * 2,
         out_specs=VMEM,
         scratch_shapes=[
             pltpu.VMEM((5, S, S), B),
@@ -366,10 +410,11 @@
             pltpu.VMEM((PAD, S), F),
             pltpu.VMEM((EP, S), F),
             pltpu.SemaphoreType.DMA((2, 7)),
+            pltpu.SemaphoreType.DMA((2, 4)),
         ],
-        compiler_params=pltpu.CompilerParams(vmem_limit_bytes=60 << 20),
+        compiler_params=pltpu.CompilerParams(vmem_limit_bytes=52 << 20),
         name="sweep",
-    )(got, prior, final, keep, other, kh, kl, mh, ml)
+    )(got, prior, final, keep, other, powers, more)
 
 
 def blend_kernel(mine, theirs, blend, out):
@@ -403,12 +448,13 @@
     swap = [(0, 1), (1, 0)]
     diag = lax.dynamic_slice_in_dim(transition, r * H, H, 1)
     recv = lax.ppermute(diag, "row", swap)
-    keep, send = innovation(obs_index, obs_visible, obs_value, gain_fwd, gain_bwd)
+    slots = jnp.stack((obs_value * obs_visible.astype(F), obs_index.astype(F)))
+    keep, send = innovation(slots, gain_fwd, gain_bwd)
     other = lax.ppermute(send, "row", swap)
-    ends, kh, kl = ladder(transition, recv, keep, other, segments)
+    ends, powers = ladder(transition, recv, keep, other, segments)
     got = lax.all_to_all(ends, "tm", 0, 0)
-    mh, ml = middle(kh, kl)
-    states = sweep(got, prior_state.reshape(1, S), final_state.reshape(1, S), keep, other, kh, kl, mh, ml)
+    more = middle(powers)
+    states = sweep(got, prior_state.reshape(1, S), final_state.reshape(1, S), keep, other, powers, more)
     theirs = lax.ppermute(states, "row", swap)
     return blended(states, theirs, blend)
 

time: 85.9 us -> 78.5 us (0.914)
  Pallas kernels: 64.6 us -> 60.6 us
  local copies, waits for them, and re-layouts: 4.85 us -> 1.48 us
    unnamed x10 -> x14, local copies, waits for them, and re-layouts: 2.59 us -> 0.03 us
    pallas_call x1, Pallas kernels: 20.6 us -> 19.1 us  [sweep(): pl.pallas_call(sweep_kernel, out_shape=jax.ShapeDtypeStruct((EP, S), F),...]
    pallas_call x1, Pallas kernels: 4.17 us -> 2.81 us  [innovation(): pl.pallas_call(innovation_kernel, out_shape=(half, half), in_specs=[VMEM,...]
    pallas_call x1, Pallas kernels: 25.4 us -> 24.1 us  [ladder(): pl.pallas_call(ladder_kernel, out_shape=(jax.ShapeDtypeStruct((segments,...]
  transfers between devices with their start and end apart: 4 -> 4, of which waited for: 2 -> 2; matrix products, arithmetic and copies ran while one was open for 0% -> 0% of each run, Pallas kernels for 20% -> 21%
where the time goes in v2:
time: 78.5 us; the launch traced here: 78.2 us
  Pallas kernels  60.6 us (77%)
  starting transfers between devices  14.1 us (18%)
  waiting for transfers between devices  1.89 us (2%)
  local copies, waits for them, and re-layouts  1.48 us (2%)
    pallas_call x1, Pallas kernels, ladder(): pl.pallas_call(ladder_kernel, out_shape=(jax.ShapeDtypeStruct((segments,...  24.1 us
    pallas_call x1, Pallas kernels, sweep(): pl.pallas_call(sweep_kernel, out_shape=jax.ShapeDtypeStruct((EP, S), F),...  19.1 us
    pallas_call x1, Pallas kernels, middle(): pl.pallas_call(middle_kernel, out_shape=jax.ShapeDtypeStruct((6, S, S), B...  13.5 us
    all_to_all x1, starting transfers between devices, per_device(): got = lax.all_to_all(ends, 'tm', 0, 0)  11.5 us
    pallas_call x1, Pallas kernels, innovation(): pl.pallas_call(innovation_kernel, out_shape=(half, half), in_specs=[VMEM,...  2.81 us
  transfers between devices with their start and end apart: 4, of which 2 were waited for; matrix products, arithmetic and copies ran while one was open for 0% of the time, Pallas kernels for 21%

profile of v2, /device:TPU:1, one launch (start us, length us, event | category | flops | bytes accessed | tf_op | source)
XLA Modules:
  0.0 78.2 jit_solution(666941412245905308)
XLA Ops:
  0.0 0.0 copy-start.1
  0.0 1.4 %constant_dynamic-slice_fusion = f32[512,512]{1,0:T(8,128)S(1)} fusion(f32[512,1024]{1,0:T(8,128)} %own.1, s32[]{:T(128)S(6)} %select_n.3), kind=kLoop, calls=%fused_computation.3 | loop fusion | bytes 2097156 | tf_op jit(solution)/shard_map/dynamic_slice | solution.py:449
  1.5 1.4 %collective-permute-start = (f32[512,512]{1,0:T(8,128)S(1)}, f32[512,512]{1,0:T(8,128)S(1)}, u32[]{:S(2)}, u32[]{:S(2)}) collective-permute-start(f32[512,512]{1,0:T(8,128)S(1)} %constant_dynamic-slice_fusion), channel_id=1, source_target_pairs={{0,1},{1,0},{2,3},{3,2},{4,5},{5,4},{6,7},{7,6},{8,9},{9,8},{10,11... | collective-permute-start | bytes 3145736 | tf_op jit(solution)/shard_map/ppermute | solution.py:450
  2.9 0.0 copy-done.6
  2.9 0.0 copy-done.4
  2.9 0.0 copy-done.5
  3.0 0.0 copy-done.1
  3.0 2.8 %innovation.1 = (f32[32,512]{1,0:T(8,128)S(1)}, f32[32,512]{1,0:T(8,128)S(1)}) custom-call(f32[2,32,128]{2,1,0:T(8,128)S(1)} %pad_maximum_fusion.slots, f32[1024,512]{1,0:T(8,128)S(1)} %copy-done.1, f32[1024,512]{1,0:T(8,128)} %gb.1), custom_call_target="tpu_custom_call" | custom-call | tf_op jit(solution)/shard_map/innovation/pallas_call | solution.py:136
  5.8 0.4 collective-permute-start.1
  6.2 0.9 %collective-permute-done.1.other = f32[32,512]{1,0:T(8,128)S(1)} collective-permute-done((f32[32,512]{1,0:T(8,128)S(1)}, f32[32,512]{1,0:T(8,128)S(1)}, u32[]{:S(2)}, u32[]{:S(2)}) %collective-permute-start.1) | collective-permute-done | bytes 65568 | tf_op jit(solution)/shard_map/ppermute | solution.py:453
  7.1 0.0 collective-permute-done.recv
  7.1 24.1 %ladder.1 = (f32[64,1,1024]{2,1,0:T(1,128)}, bf16[10,1024,1024]{2,1,0:T(8,128)(2,1)}) custom-call(f32[512,1024]{1,0:T(8,128)} %own.1, f32[512,512]{1,0:T(8,128)S(1)} %collective-permute-done.recv, f32[32,512]{1,0:T(8,128)S(1)} %get-tuple-element.9.keep, f32[32,512]{1,0:T(8,128)S(1)} %collective-permute-done.1.other), custom_call_target="tpu_custom_call" | custom-call | tf_op jit(solution)/shard_map/ladder/pallas_call | solution.py:227
  31.3 11.5 %all-to-all-start = ((f32[64,1,1024]{2,1,0:T(1,128)}), f32[64,1,1024]{2,1,0:T(1,128)S(1)}, u32[]{:S(2)}, u32[]{:S(2)}) async-start(f32[64,1,1024]{2,1,0:T(1,128)} %get-tuple-element.11), calls=%async_computation | async-start | bytes 524288 | tf_op jit(solution)/shard_map/all_to_all | solution.py:455
  42.8 0.0 copy-start.2
  42.8 0.0 copy-start.3
  42.8 13.5 %middle.1.more = bf16[6,1024,1024]{2,1,0:T(8,128)(2,1)} custom-call(bf16[10,1024,1024]{2,1,0:T(8,128)(2,1)} %get-tuple-element.12.powers), custom_call_target="tpu_custom_call" | custom-call | tf_op jit(solution)/shard_map/middle/pallas_call | solution.py:285
  56.3 0.0 all-to-all-done.got
  56.3 0.0 copy-done.2
  56.3 0.0 copy-done.3
  56.3 0.0 copy-start
  56.3 19.1 %sweep.1.mine = f32[32,1024]{1,0:T(8,128)S(1)} custom-call(f32[64,1,1024]{2,1,0:T(1,128)S(1)} %all-to-all-done.got, f32[1,1024]{1,0:T(1,128)S(1)} %bitcast.6, f32[1,1024]{1,0:T(1,128)S(1)} %bitcast.7, f32[32,512]{1,0:T(8,128)S(1)} %get-tuple-element.9.keep, f32[32,512]{1,0:T(8,128)S(1)} %collective-permute-done.1.other, ...), custom_call_target="tpu_custom_call" | custom-call | tf_op jit(solution)/shard_map/sweep/pallas_call | solution.py:396
  75.4 0.7 collective-permute-start.2
  76.1 1.0 %collective-permute-done.2.theirs = f32[32,1024]{1,0:T(8,128)S(1)} collective-permute-done((f32[32,1024]{1,0:T(8,128)S(1)}, f32[32,1024]{1,0:T(8,128)S(1)}, u32[]{:S(2)}, u32[]{:S(2)}) %collective-permute-start.2) | collective-permute-done | bytes 131104 | tf_op jit(solution)/shard_map/ppermute | solution.py:458
  77.1 1.1 %blended.1 = f32[32,512]{1,0:T(8,128)} custom-call(f32[32,1024]{1,0:T(8,128)S(1)} %sweep.1.mine, f32[32,1024]{1,0:T(8,128)S(1)} %collective-permute-done.2.theirs, f32[1024,512]{1,0:T(8,128)S(1)} %copy-done), custom_call_target="tpu_custom_call" | custom-call | tf_op jit(solution)/shard_map/blended/pallas_call | solution.py:435
  (7 shorter events, 0.0 us)
Async XLA Ops:
  0.0 2.9 %copy-start.6 = (s32[32,128]{1,0:T(8,128)S(1)}, s32[32,128]{1,0:T(8,128)}, u32[]{:S(2)}) copy-start(s32[32,128]{1,0:T(8,128)} %param.15) | copy-start | bytes 49156
  0.0 2.9 %copy-start.4 = (f32[32,128]{1,0:T(8,128)S(1)}, f32[32,128]{1,0:T(8,128)}, u32[]{:S(2)}) copy-start(f32[32,128]{1,0:T(8,128)} %param.17) | copy-start | bytes 49156
  0.0 2.9 %copy-start.5 = (s32[32,128]{1,0:T(8,128)S(1)}, s32[32,128]{1,0:T(8,128)}, u32[]{:S(2)}) copy-start(s32[32,128]{1,0:T(8,128)} %param.16) | copy-start | bytes 49156
  0.0 3.0 %copy-start.1 = (f32[1024,512]{1,0:T(8,128)S(1)}, f32[1024,512]{1,0:T(8,128)}, u32[]{:S(2)}) copy-start(f32[1024,512]{1,0:T(8,128)} %gf.1) | copy-start | bytes 6291460
  1.5 5.7 %collective-permute-start = (f32[512,512]{1,0:T(8,128)S(1)}, f32[512,512]{1,0:T(8,128)S(1)}, u32[]{:S(2)}, u32[]{:S(2)}) collective-permute-start(f32[512,512]{1,0:T(8,128)S(1)} %constant_dynamic-slice_fusion), channel_id=1, source_target_pairs={{0,1},{1,0},{2,3},{3,2},{4,5},{5,4},{6,7},{7,6},{8,9},{9,8},{10,11... | collective-permute-start | bytes 3145736 | tf_op jit(solution)/shard_map/ppermute | solution.py:450
  5.8 1.3 %collective-permute-start.1 = (f32[32,512]{1,0:T(8,128)S(1)}, f32[32,512]{1,0:T(8,128)S(1)}, u32[]{:S(2)}, u32[]{:S(2)}) collective-permute-start(f32[32,512]{1,0:T(8,128)S(1)} %get-tuple-element.10), channel_id=1, source_target_pairs={{0,1},{1,0},{2,3},{3,2},{4,5},{5,4},{6,7},{7,6},{8,9},{9,8},{10,11... | collective-permute-start | bytes 196616 | tf_op jit(solution)/shard_map/ppermute | solution.py:453
  31.3 25.0 %all-to-all-start = ((f32[64,1,1024]{2,1,0:T(1,128)}), f32[64,1,1024]{2,1,0:T(1,128)S(1)}, u32[]{:S(2)}, u32[]{:S(2)}) async-start(f32[64,1,1024]{2,1,0:T(1,128)} %get-tuple-element.11), calls=%async_computation | async-start | bytes 524288 | tf_op jit(solution)/shard_map/all_to_all | solution.py:455
  42.8 13.5 %copy-start.2 = (f32[1024]{0:T(1024)S(1)}, f32[1024]{0:T(1024)}, u32[]{:S(2)}) copy-start(f32[1024]{0:T(1024)} %param.13) | copy-start | bytes 12292
  42.8 13.5 %copy-start.3 = (f32[1024]{0:T(1024)S(1)}, f32[1024]{0:T(1024)}, u32[]{:S(2)}) copy-start(f32[1024]{0:T(1024)} %param.14) | copy-start | bytes 12292
  56.3 20.8 %copy-start = (f32[1024,512]{1,0:T(8,128)S(1)}, f32[1024,512]{1,0:T(8,128)}, u32[]{:S(2)}) copy-start(f32[1024,512]{1,0:T(8,128)} %blend.1) | copy-start | bytes 6291460
  75.4 1.7 %collective-permute-start.2 = (f32[32,1024]{1,0:T(8,128)S(1)}, f32[32,1024]{1,0:T(8,128)S(1)}, u32[]{:S(2)}, u32[]{:S(2)}) collective-permute-start(f32[32,1024]{1,0:T(8,128)S(1)} %sweep.1.mine), channel_id=1, source_target_pairs={{0,1},{1,0},{2,3},{3,2},{4,5},{5,4},{6,7},{7,6},{8,9},{9,8},{10,11... | collective-permute-start | bytes 393224 | tf_op jit(solution)/shard_map/ppermute | solution.py:458

commit v3 on v2

--- a/solution.py
+++ b/solution.py
@@ -230,7 +230,7 @@
         out_specs=(VMEM, HBM),
         scratch_shapes=[slab, slab, full, slab, slab, full]
         + [pltpu.VMEM((EP, S), F), pltpu.VMEM((PAD, S), F), pltpu.SemaphoreType.DMA((16,))],
-        compiler_params=pltpu.CompilerParams(vmem_limit_bytes=52 << 20),
+        compiler_params=pltpu.CompilerParams(vmem_limit_bytes=40 << 20),
         name="ladder",
     )(own, recv, keep, other)
 

time: 78.5 us -> 76.9 us (0.980)
  Pallas kernels: 60.6 us -> 59.1 us
    pallas_call x1, Pallas kernels: 24.1 us -> 22.6 us  [ladder(): pl.pallas_call(ladder_kernel, out_shape=(jax.ShapeDtypeStruct((segments,...]
where the time goes in v3:
time: 76.9 us; the launch traced here: 76.7 us
  Pallas kernels  59.1 us (77%)
  starting transfers between devices  14 us (18%)
  waiting for transfers between devices  1.9 us (2%)
  local copies, waits for them, and re-layouts  1.49 us (2%)
    pallas_call x1, Pallas kernels, ladder(): pl.pallas_call(ladder_kernel, out_shape=(jax.ShapeDtypeStruct((segments,...  22.6 us
    pallas_call x1, Pallas kernels, sweep(): pl.pallas_call(sweep_kernel, out_shape=jax.ShapeDtypeStruct((EP, S), F),...  19.1 us
    pallas_call x1, Pallas kernels, middle(): pl.pallas_call(middle_kernel, out_shape=jax.ShapeDtypeStruct((6, S, S), B...  13.5 us
    all_to_all x1, starting transfers between devices, per_device(): got = lax.all_to_all(ends, 'tm', 0, 0)  11.5 us
    pallas_call x1, Pallas kernels, innovation(): pl.pallas_call(innovation_kernel, out_shape=(half, half), in_specs=[VMEM,...  2.81 us
  transfers between devices with their start and end apart: 4, of which 2 were waited for; matrix products, arithmetic and copies ran while one was open for 0% of the time, Pallas kernels for 21%

profile of v3, /device:TPU:1, one launch (start us, length us, event | category | flops | bytes accessed | tf_op | source)
XLA Modules:
  0.0 76.7 jit_solution(13535386557962014782)
XLA Ops:
  0.0 0.0 copy-start.2
  0.0 1.4 %constant_dynamic-slice_fusion = f32[512,512]{1,0:T(8,128)S(1)} fusion(f32[512,1024]{1,0:T(8,128)} %own.1, s32[]{:T(128)S(6)} %select_n.3), kind=kLoop, calls=%fused_computation.3 | loop fusion | bytes 2097156 | tf_op jit(solution)/shard_map/dynamic_slice | solution.py:449
  1.5 1.4 %collective-permute-start = (f32[512,512]{1,0:T(8,128)S(1)}, f32[512,512]{1,0:T(8,128)S(1)}, u32[]{:S(2)}, u32[]{:S(2)}) collective-permute-start(f32[512,512]{1,0:T(8,128)S(1)} %constant_dynamic-slice_fusion), channel_id=1, source_target_pairs={{0,1},{1,0},{2,3},{3,2},{4,5},{5,4},{6,7},{7,6},{8,9},{9,8},{10,11... | collective-permute-start | bytes 3145736 | tf_op jit(solution)/shard_map/ppermute | solution.py:450
  2.9 0.0 copy-done.7
  2.9 0.0 copy-done.5
  2.9 0.0 copy-done.6
  3.0 0.0 copy-done.2
  3.0 0.0 copy-start
  3.0 2.8 %innovation.1 = (f32[32,512]{1,0:T(8,128)S(1)}, f32[32,512]{1,0:T(8,128)S(1)}) custom-call(f32[2,32,128]{2,1,0:T(8,128)S(1)} %pad_maximum_fusion.slots, f32[1024,512]{1,0:T(8,128)S(1)} %copy-done.2, f32[1024,512]{1,0:T(8,128)} %gb.1), custom_call_target="tpu_custom_call" | custom-call | tf_op jit(solution)/shard_map/innovation/pallas_call | solution.py:136
  5.8 0.4 collective-permute-start.1
  6.2 0.9 %collective-permute-done.1.other = f32[32,512]{1,0:T(8,128)S(1)} collective-permute-done((f32[32,512]{1,0:T(8,128)S(1)}, f32[32,512]{1,0:T(8,128)S(1)}, u32[]{:S(2)}, u32[]{:S(2)}) %collective-permute-start.1) | collective-permute-done | bytes 65568 | tf_op jit(solution)/shard_map/ppermute | solution.py:453
  7.1 0.0 collective-permute-done.recv
  7.1 0.0 copy-done
  7.1 22.6 %ladder.1 = (f32[64,1,1024]{2,1,0:T(1,128)}, bf16[10,1024,1024]{2,1,0:T(8,128)(2,1)}) custom-call(f32[512,1024]{1,0:T(8,128)S(1)} %copy-done, f32[512,512]{1,0:T(8,128)S(1)} %collective-permute-done.recv, f32[32,512]{1,0:T(8,128)S(1)} %get-tuple-element.9.keep, f32[32,512]{1,0:T(8,128)S(1)} %collective-permute-done.1.other), custom_call_target="tpu_custom_call" | custom-call | tf_op jit(solution)/shard_map/ladder/pallas_call | solution.py:227
  29.7 11.5 %all-to-all-start = ((f32[64,1,1024]{2,1,0:T(1,128)}), f32[64,1,1024]{2,1,0:T(1,128)S(1)}, u32[]{:S(2)}, u32[]{:S(2)}) async-start(f32[64,1,1024]{2,1,0:T(1,128)} %get-tuple-element.11), calls=%async_computation | async-start | bytes 524288 | tf_op jit(solution)/shard_map/all_to_all | solution.py:455
  41.2 0.0 copy-start.3
  41.2 0.0 copy-start.4
  41.3 13.5 %middle.1.more = bf16[6,1024,1024]{2,1,0:T(8,128)(2,1)} custom-call(bf16[10,1024,1024]{2,1,0:T(8,128)(2,1)} %get-tuple-element.12.powers), custom_call_target="tpu_custom_call" | custom-call | tf_op jit(solution)/shard_map/middle/pallas_call | solution.py:285
  54.7 0.0 all-to-all-done.got
  54.8 0.0 copy-start.1
  54.8 19.1 %sweep.1.mine = f32[32,1024]{1,0:T(8,128)S(1)} custom-call(f32[64,1,1024]{2,1,0:T(1,128)S(1)} %all-to-all-done.got, f32[1,1024]{1,0:T(1,128)S(1)} %bitcast.6, f32[1,1024]{1,0:T(1,128)S(1)} %bitcast.7, f32[32,512]{1,0:T(8,128)S(1)} %get-tuple-element.9.keep, f32[32,512]{1,0:T(8,128)S(1)} %collective-permute-done.1.other, ...), custom_call_target="tpu_custom_call" | custom-call | tf_op jit(solution)/shard_map/sweep/pallas_call | solution.py:396
  73.9 0.7 collective-permute-start.2
  74.5 1.0 %collective-permute-done.2.theirs = f32[32,1024]{1,0:T(8,128)S(1)} collective-permute-done((f32[32,1024]{1,0:T(8,128)S(1)}, f32[32,1024]{1,0:T(8,128)S(1)}, u32[]{:S(2)}, u32[]{:S(2)}) %collective-permute-start.2) | collective-permute-done | bytes 131104 | tf_op jit(solution)/shard_map/ppermute | solution.py:458
  75.5 1.2 %blended.1 = f32[32,512]{1,0:T(8,128)} custom-call(f32[32,1024]{1,0:T(8,128)S(1)} %sweep.1.mine, f32[32,1024]{1,0:T(8,128)S(1)} %collective-permute-done.2.theirs, f32[1024,512]{1,0:T(8,128)S(1)} %copy-done.1), custom_call_target="tpu_custom_call" | custom-call | tf_op jit(solution)/shard_map/blended/pallas_call | solution.py:435
  (9 shorter events, 0.0 us)
Async XLA Ops:
  0.0 2.9 %copy-start.7 = (s32[32,128]{1,0:T(8,128)S(1)}, s32[32,128]{1,0:T(8,128)}, u32[]{:S(2)}) copy-start(s32[32,128]{1,0:T(8,128)} %param.15) | copy-start | bytes 49156
  0.0 2.9 %copy-start.5 = (f32[32,128]{1,0:T(8,128)S(1)}, f32[32,128]{1,0:T(8,128)}, u32[]{:S(2)}) copy-start(f32[32,128]{1,0:T(8,128)} %param.17) | copy-start | bytes 49156
  0.0 2.9 %copy-start.6 = (s32[32,128]{1,0:T(8,128)S(1)}, s32[32,128]{1,0:T(8,128)}, u32[]{:S(2)}) copy-start(s32[32,128]{1,0:T(8,128)} %param.16) | copy-start | bytes 49156
  0.0 3.0 %copy-start.2 = (f32[1024,512]{1,0:T(8,128)S(1)}, f32[1024,512]{1,0:T(8,128)}, u32[]{:S(2)}) copy-start(f32[1024,512]{1,0:T(8,128)} %gf.1) | copy-start | bytes 6291460
  1.5 5.7 %collective-permute-start = (f32[512,512]{1,0:T(8,128)S(1)}, f32[512,512]{1,0:T(8,128)S(1)}, u32[]{:S(2)}, u32[]{:S(2)}) collective-permute-start(f32[512,512]{1,0:T(8,128)S(1)} %constant_dynamic-slice_fusion), channel_id=1, source_target_pairs={{0,1},{1,0},{2,3},{3,2},{4,5},{5,4},{6,7},{7,6},{8,9},{9,8},{10,11... | collective-permute-start | bytes 3145736 | tf_op jit(solution)/shard_map/ppermute | solution.py:450
  3.0 4.2 %copy-start = (f32[512,1024]{1,0:T(8,128)S(1)}, f32[512,1024]{1,0:T(8,128)}, u32[]{:S(2)}) copy-start(f32[512,1024]{1,0:T(8,128)} %own.1) | copy-start | bytes 6291460
  5.8 1.3 %collective-permute-start.1 = (f32[32,512]{1,0:T(8,128)S(1)}, f32[32,512]{1,0:T(8,128)S(1)}, u32[]{:S(2)}, u32[]{:S(2)}) collective-permute-start(f32[32,512]{1,0:T(8,128)S(1)} %get-tuple-element.10), channel_id=1, source_target_pairs={{0,1},{1,0},{2,3},{3,2},{4,5},{5,4},{6,7},{7,6},{8,9},{9,8},{10,11... | collective-permute-start | bytes 196616 | tf_op jit(solution)/shard_map/ppermute | solution.py:453
  29.7 25.0 %all-to-all-start = ((f32[64,1,1024]{2,1,0:T(1,128)}), f32[64,1,1024]{2,1,0:T(1,128)S(1)}, u32[]{:S(2)}, u32[]{:S(2)}) async-start(f32[64,1,1024]{2,1,0:T(1,128)} %get-tuple-element.11), calls=%async_computation | async-start | bytes 524288 | tf_op jit(solution)/shard_map/all_to_all | solution.py:455
  41.2 13.5 %copy-start.3 = (f32[1024]{0:T(1024)S(1)}, f32[1024]{0:T(1024)}, u32[]{:S(2)}) copy-start(f32[1024]{0:T(1024)} %param.13) | copy-start | bytes 12292
  41.2 13.5 %copy-start.4 = (f32[1024]{0:T(1024)S(1)}, f32[1024]{0:T(1024)}, u32[]{:S(2)}) copy-start(f32[1024]{0:T(1024)} %param.14) | copy-start | bytes 12292
  54.8 20.8 %copy-start.1 = (f32[1024,512]{1,0:T(8,128)S(1)}, f32[1024,512]{1,0:T(8,128)}, u32[]{:S(2)}) copy-start(f32[1024,512]{1,0:T(8,128)} %blend.1) | copy-start | bytes 6291460
  73.9 1.7 %collective-permute-start.2 = (f32[32,1024]{1,0:T(8,128)S(1)}, f32[32,1024]{1,0:T(8,128)S(1)}, u32[]{:S(2)}, u32[]{:S(2)}) collective-permute-start(f32[32,1024]{1,0:T(8,128)S(1)} %sweep.1.mine), channel_id=1, source_target_pairs={{0,1},{1,0},{2,3},{3,2},{4,5},{5,4},{6,7},{7,6},{8,9},{9,8},{10,11... | collective-permute-start | bytes 393224 | tf_op jit(solution)/shard_map/ppermute | solution.py:458
